TPU v7x, 256 devices: a whole 4x4x8 slice. The times are simulated.
256 devices in a mesh: row: 16 (over y_lo, x, core), col: 16 (over y_hi, z).
Axes of the slice: x: 4, y: 4 (y_hi: 2, y_lo: 2; y = y_hi * 2 + y_lo), z: 8, core: 2. Of those that a mesh axis runs over, the one named last changes fastest.
Arguments:
- tokens: bfloat16 [512, 12288], P('row', 'col'), may hold values from -6 to 6
- out_grad: bfloat16 [512, 12288], P('row', 'col'), may hold values from -6 to 6
- w_in: bfloat16 [12288, 24576], P('col', 'row'), may hold values from -0.0546875 to 0.0546875
- w_out: bfloat16 [24576, 12288], P('row', 'col'), may hold values from -0.0390625 to 0.0390625
- bias_in: float32 [24576], P('row'), may hold values from -3 to 3
- stream_ids: int32 [3], replicated, may hold values from 0 to 4095
- tile_keys: int32 [64, 192], replicated, may hold values from 0 to 16777215
Outputs:
- grad_tokens: bfloat16 [512, 12288], P('row', 'col')
- grad_w_in: bfloat16 [12288, 24576], P('col', 'row')
- grad_w_out: bfloat16 [24576, 12288], P('row', 'col')
- grad_bias_in: float32 [24576], P('row')
- grad_bias_out: float32 [12288], P('col')
All inputs are finite; a program needn't handle non-finite values.
Results may differ from a plain program's by a relative error of at most 0.005.
Values may be sent and summed in bfloat16 or wider, within the bound.
No kernel may reach another device: no remote copies, remote signals or barrier semaphores. Data moves between devices by JAX's collectives and lax.ppermute only.
A program may use at most 64 MiB of HBM per device.

v0:
```python
import jax
import jax.numpy as jnp
from jax import lax
from jax.sharding import PartitionSpec as P

TILE_T = 8
TILE_F = 128
mix_one = 73856093
mix_two = 19349663
mix_three = 83492791
golden = -1640531535
mult_one = 2146121005
mult_two = -2073254261


def shift_down(value, count):
    return lax.shift_right_logical(value, jnp.full(value.shape, count, jnp.int32))


def keep_mask(tile_keys, stream_ids, row_start, row_count, col_start, col_count, tile_t, tile_f):
    row_ids = row_start + jnp.arange(row_count, dtype=jnp.int32)
    col_ids = col_start + jnp.arange(col_count, dtype=jnp.int32)
    onehot_rows = (
        row_ids[:, None] // tile_t == jnp.arange(tile_keys.shape[0], dtype=jnp.int32)[None, :]
    ).astype(jnp.int32)
    onehot_cols = (
        jnp.arange(tile_keys.shape[1], dtype=jnp.int32)[:, None] == col_ids[None, :] // tile_f
    ).astype(jnp.int32)
    picked = jnp.dot(onehot_rows, tile_keys, preferred_element_type=jnp.int32)
    picked = jnp.dot(picked, onehot_cols, preferred_element_type=jnp.int32)
    salt = (
        stream_ids[0] * jnp.int32(mix_one)
        ^ stream_ids[1] * jnp.int32(mix_two)
        ^ stream_ids[2] * jnp.int32(mix_three)
    )
    offset = row_ids[:, None] % tile_t * tile_f + col_ids[None, :] % tile_f
    value = (picked ^ salt) + offset * jnp.int32(golden)
    value = value ^ shift_down(value, 16)
    value = value * jnp.int32(mult_one)
    value = value ^ shift_down(value, 15)
    value = value * jnp.int32(mult_two)
    value = value ^ shift_down(value, 16)
    return (shift_down(value, 8) & jnp.int32(1023) < jnp.int32(922)).astype(jnp.float32)


def normal_cdf(value):
    return 0.5 * (1.0 + lax.erf(value * 0.7071067811865476))


def local_gelu(pre_part, dact_part, bias_part, keep):
    pre = pre_part + bias_part
    scaled = keep * (1.0 / 0.9)
    cdf = normal_cdf(pre)
    act = (pre * cdf * scaled).astype(jnp.bfloat16)
    slope = cdf + pre * jnp.exp(-0.5 * pre * pre) * 0.3989422804014327
    dpre = (dact_part * scaled * slope).astype(jnp.bfloat16)
    return (act, dpre)


def local(tokens, out_grad, w_in, w_out, bias_in, stream_ids, tile_keys):
    col_count = lax.axis_size("col")
    row_index = lax.axis_index("row")
    col_index = lax.axis_index("col")
    ff_local = w_in.shape[1]
    all_tokens, all_grads = (
        lax.all_gather(tokens, "row", axis=0, tiled=True),
        lax.all_gather(out_grad, "row", axis=0, tiled=True),
    )
    total_tokens = all_tokens.shape[0]
    pre_terms = jnp.dot(all_tokens, w_in, preferred_element_type=jnp.float32)
    dact_terms = lax.dot_general(
        all_grads, w_out, (((1,), (1,)), ((), ())), preferred_element_type=jnp.float32
    )
    pre_part, dact_part = (
        lax.psum_scatter(pre_terms, "col", scatter_dimension=0, tiled=True),
        lax.psum_scatter(dact_terms, "col", scatter_dimension=0, tiled=True),
    )
    height = total_tokens // col_count
    keep = keep_mask(
        tile_keys,
        stream_ids,
        col_index * height,
        height,
        row_index * ff_local,
        ff_local,
        TILE_T,
        TILE_F,
    )
    act, dpre = local_gelu(pre_part, dact_part, bias_in[None, :], keep)
    act_all, dpre_all = (
        lax.all_gather(act, "col", axis=0, tiled=True),
        lax.all_gather(dpre, "col", axis=0, tiled=True),
    )
    grad_w_out = lax.dot_general(
        act_all, all_grads, (((0,), (0,)), ((), ())), preferred_element_type=jnp.float32
    ).astype(jnp.bfloat16)
    grad_w_in = lax.dot_general(
        all_tokens, dpre_all, (((0,), (0,)), ((), ())), preferred_element_type=jnp.float32
    ).astype(jnp.bfloat16)
    grad_tokens = lax.psum_scatter(
        lax.dot_general(
            dpre_all, w_in, (((1,), (1,)), ((), ())), preferred_element_type=jnp.float32
        ),
        "row",
        scatter_dimension=0,
        tiled=True,
    ).astype(jnp.bfloat16)
    grad_bias_in = jnp.sum(dpre_all.astype(jnp.float32), axis=0)
    grad_bias_out = jnp.sum(all_grads.astype(jnp.float32), axis=0)
    return (grad_tokens, grad_w_in, grad_w_out, grad_bias_in, grad_bias_out)


def solution(mesh):
    return jax.shard_map(
        local,
        mesh=mesh,
        in_specs=(
            P("row", "col"),
            P("row", "col"),
            P("col", "row"),
            P("row", "col"),
            P("row"),
            P(),
            P(),
        ),
        out_specs=(P("row", "col"), P("col", "row"), P("row", "col"), P("row"), P("col")),
        check_vma=False,
    )
```

profile of v0, /device:TPU:32, one launch (start us, length us, event | category | flops | bytes accessed | tf_op | source)
XLA Modules:
  0.0 694.8 jit_solution(11404582454193071969)
XLA Ops:
  7.2 0.0 copy-start
  7.2 0.0 reduce-scatter.6.cloned.1.call-start
  7.2 22.2 %all_gather.13 = bf16[512,768]{1,0:T(8,128)(2,1)S(1)} all-gather(bf16[32,768]{1,0:T(8,128)(2,1)} %param.7), channel_id=1, replica_groups=mesh['row'=16,'col'=16] {'row'}, dimensions={0}, use_global_device_ids=true | all-gather | bytes 835584 | tf_op jit(solution)/shard_map/all_gather | solution.py:66
  29.4 0.0 copy-done
  29.5 0.0 copy-start.1
  29.5 3.0 fusion.45
  32.5 0.0 copy-done.1
  32.5 0.0 copy-start.2
  32.5 0.0 reduce-scatter.6.cloned.1.call-update
  32.5 0.0 reduce-scatter.4.cloned.1.call-start
  32.6 0.7 copy-done.2
  33.3 18.4 %all_gather.12 = bf16[512,768]{1,0:T(8,128)(2,1)S(1)} all-gather(bf16[32,768]{1,0:T(8,128)(2,1)S(1)} %copy-done.2), channel_id=1, replica_groups=mesh['row'=16,'col'=16] {'row'}, dimensions={0}, use_global_device_ids=true | all-gather | bytes 835584 | tf_op jit(solution)/shard_map/all_gather | solution.py:67
  51.7 4.8 fusion.44
  56.5 0.0 copy-start.3
  56.5 0.0 copy-start.4
  56.5 0.0 copy-start.5
  56.5 0.0 reduce-scatter.4.cloned.1.call-update
  56.5 0.0 all-gather.3.cloned.1.call-start
  56.5 0.6 copy-done.3
  57.1 0.6 fusion.43
  59.7 183.7 %reduce-scatter.6.cloned.1.call-done = f32[32,1536]{1,0:T(8,128)} async-done(((f32[512,1536]{1,0:T(8,128)}), f32[32,1536]{1,0:T(8,128)}) %reduce-scatter.6.cloned.1.call-update) | async-done | bytes 196624 | tf_op jit(solution)/shard_map/reduce_scatter | solution.py:75
  243.4 213.6 %reduce-scatter.4.cloned.1.call-done = f32[32,1536]{1,0:T(8,128)} async-done(((f32[512,1536]{1,0:T(8,128)}), f32[32,1536]{1,0:T(8,128)}) %reduce-scatter.4.cloned.1.call-update) | async-done | bytes 196624 | tf_op jit(solution)/shard_map/reduce_scatter | solution.py:76
  457.0 0.0 copy-done.4
  457.0 0.0 copy-done.5
  457.0 2.6 multiply_convert_fusion
  459.6 0.0 all-gather.3.cloned.1.call-update
  459.6 0.0 all-gather.5.cloned.1.call-start
  459.7 0.5 all-gather.5.cloned.1.call-update
  460.2 0.0 reduce-scatter.8.cloned.1.call-start
  460.2 80.2 %all-gather.3.cloned.1.call-done = bf16[512,1536]{1,0:T(8,128)(2,1)} async-done(((bf16[32,1536]{1,0:T(8,128)(2,1)}), bf16[512,1536]{1,0:T(8,128)(2,1)}) %all-gather.3.cloned.1.call-update) | async-done | bytes 1572880 | tf_op jit(solution)/shard_map/all_gather | solution.py:92
  540.5 4.0 fusion.46
  544.4 0.0 reduce-scatter.8.cloned.1.call-update
  544.5 0.7 convert_reduce_fusion.1
  545.2 4.4 fusion
  549.6 4.3 copy.12
  553.9 2.3 convert_reduce_fusion
  556.2 65.3 %all-gather.5.cloned.1.call-done = bf16[512,1536]{1,0:T(8,128)(2,1)} async-done(((bf16[32,1536]{1,0:T(8,128)(2,1)}), bf16[512,1536]{1,0:T(8,128)(2,1)}) %all-gather.5.cloned.1.call-update) | async-done | bytes 1572880 | tf_op jit(solution)/shard_map/all_gather | solution.py:91
  621.5 4.2 convolution_convert_fusion
  625.7 61.0 %reduce-scatter.8.cloned.1.call-done = f32[32,768]{1,0:T(8,128)} async-done(((f32[512,768]{1,0:T(8,128)}), f32[32,768]{1,0:T(8,128)}) %reduce-scatter.8.cloned.1.call-update) | async-done | bytes 98320 | tf_op jit(solution)/shard_map/reduce_scatter | solution.py:100
  686.7 1.5 convert_element_type.28
  (2 shorter events, 0.0 us)
Async XLA Ops:
  7.2 22.3 %copy-start = (bf16[768,1536]{1,0:T(8,128)(2,1)S(1)}, bf16[768,1536]{1,0:T(8,128)(2,1)}, u32[]{:S(2)}) copy-start(bf16[768,1536]{1,0:T(8,128)(2,1)} %param.9) | copy-start | bytes 7077892
  7.2 236.2 %reduce-scatter.6.cloned.1.call-start = ((), (), s32[]{:S(2)}) async-start(), calls=%async_computation.4 | async-start | bytes 3342336 | tf_op jit(solution)/shard_map/reduce_scatter | solution.py:75
  29.5 3.0 copy-start.1
  32.5 0.8 copy-start.2
  32.5 424.5 %reduce-scatter.4.cloned.1.call-start = ((), (), s32[]{:S(2)}) async-start(), calls=%async_computation.3 | async-start | bytes 3342336 | tf_op jit(solution)/shard_map/reduce_scatter | solution.py:76
  56.5 0.7 copy-start.3
  56.5 400.5 %copy-start.4 = (s32[64,192]{1,0:T(8,128)S(1)}, s32[64,192]{1,0:T(8,128)}, u32[]{:S(2)}) copy-start(s32[64,192]{1,0:T(8,128)} %param.13) | copy-start | bytes 147460
  56.5 400.5 %copy-start.5 = (f32[1536]{0:T(1024)S(1)}, f32[1536]{0:T(1024)}, u32[]{:S(2)}) copy-start(f32[1536]{0:T(1024)} %param.11) | copy-start | bytes 18436
  56.5 484.0 %all-gather.3.cloned.1.call-start = ((), (), s32[]{:S(2)}) async-start(), calls=%async_computation.5 | async-start | bytes 1671168 | tf_op jit(solution)/shard_map/all_gather | solution.py:92
  459.6 161.9 %all-gather.5.cloned.1.call-start = ((), (), s32[]{:S(2)}) async-start(), calls=%async_computation.7 | async-start | bytes 1671168 | tf_op jit(solution)/shard_map/all_gather | solution.py:91
  460.2 226.6 %reduce-scatter.8.cloned.1.call-start = ((), (), s32[]{:S(2)}) async-start(), calls=%async_computation.6 | async-start | bytes 1671168 | tf_op jit(solution)/shard_map/reduce_scatter | solution.py:100
Sparse Core Ops, SparseCore 0:
  32.6 210.7 reduce-scatter.5
  247.4 209.5 reduce-scatter.3
  460.2 80.2 all-gather.2
  542.9 78.5 all-gather.4
  623.9 62.8 reduce-scatter.7
where the time goes:
time: 695 us
  waiting for transfers between devices  604 us (87%)
  blocking collectives  40.6 us (6%)
  matrix products  23 us (3%)
  between operations  15.8 us (2%)
    reduce_scatter x1, waiting for transfers between devices, local(): lax.psum_scatter(dact_terms, 'col', scatter_dimension=0, tiled=True)  214 us
    reduce_scatter x1, waiting for transfers between devices, local(): lax.psum_scatter(pre_terms, 'col', scatter_dimension=0, tiled=True)  184 us
    all_gather x1, waiting for transfers between devices, local(): lax.all_gather(dpre, 'col', axis=0, tiled=True)  80.2 us
    all_gather x1, waiting for transfers between devices, local(): lax.all_gather(act, 'col', axis=0, tiled=True)  65.3 us
    reduce_scatter x1, waiting for transfers between devices, local(): lax.psum_scatter(lax.dot_general(dpre_all, w_in, (((1,), (1,)), ((), ()))...  61 us
    all_gather x1, blocking collectives, local(): lax.all_gather(tokens, 'row', axis=0, tiled=True)  22.2 us
    all_gather x1, blocking collectives, local(): lax.all_gather(out_grad, 'row', axis=0, tiled=True)  18.4 us
  transfers between devices with their start and end apart: 5, of which 5 were waited for; matrix products, arithmetic and copies ran while one was open for 4% of the time, Pallas kernels for 0%

commit v1 on v0

--- a/solution.py
+++ b/solution.py
@@ -89,7 +89,15 @@
     act, dpre = local_gelu(pre_part, dact_part, bias_in[None, :], keep)
     act_all, dpre_all = (
         lax.all_gather(act, "col", axis=0, tiled=True),
-        lax.all_gather(dpre, "col", axis=0, tiled=True),
+        jnp.concatenate(
+            jax.lax.all_to_all(
+                jnp.stack([dpre for _ in range(jax.lax.axis_size("col"))], axis=0),
+                axis_name="col",
+                split_axis=0,
+                concat_axis=0,
+            ),
+            axis=0,
+        ),
     )
     grad_w_out = lax.dot_general(
         act_all, all_grads, (((0,), (0,)), ((), ())), preferred_element_type=jnp.float32

time: 695 us -> 630 us (0.906)
  waiting for transfers between devices: 604 us -> 530 us
    all_gather x1 -> x0, waiting for transfers between devices: 80.2 us -> none  [local(): lax.all_gather(dpre, 'col', axis=0, tiled=True)]
    all_to_all x0 -> x1, waiting for transfers between devices: none -> 36.2 us  [local(): jax.lax.all_to_all(jnp.stack([dpre for _ in range(jax.lax.axis_size('col'...]
    all_gather x1, waiting for transfers between devices: 65.3 us -> 35.2 us  [local(): lax.all_gather(act, 'col', axis=0, tiled=True)]
where the time goes in v1:
time: 630 us; the launch traced here: 629 us
  waiting for transfers between devices  530 us (84%)
  blocking collectives  40.6 us (6%)
  matrix products  23 us (4%)
  between operations  15.8 us (3%)
  local copies, waits for them, and re-layouts  7.51 us (1%)
  starting transfers between devices  7.03 us (1%)
    reduce_scatter x1, waiting for transfers between devices, local(): lax.psum_scatter(dact_terms, 'col', scatter_dimension=0, tiled=True)  214 us
    reduce_scatter x1, waiting for transfers between devices, local(): lax.psum_scatter(pre_terms, 'col', scatter_dimension=0, tiled=True)  184 us
    reduce_scatter x1, waiting for transfers between devices, local(): lax.psum_scatter(lax.dot_general(dpre_all, w_in, (((1,), (1,)), ((), ()))...  61 us
    all_to_all x1, waiting for transfers between devices, local(): jax.lax.all_to_all(jnp.stack([dpre for _ in range(jax.lax.axis_size('col'...  36.2 us
    all_gather x1, waiting for transfers between devices, local(): lax.all_gather(act, 'col', axis=0, tiled=True)  35.2 us
    all_gather x1, blocking collectives, local(): lax.all_gather(tokens, 'row', axis=0, tiled=True)  22.2 us
    all_gather x1, blocking collectives, local(): lax.all_gather(out_grad, 'row', axis=0, tiled=True)  18.4 us
  transfers between devices with their start and end apart: 5, of which 5 were waited for; matrix products, arithmetic and copies ran while one was open for 4% of the time, Pallas kernels for 0%

profile of v1, /device:TPU:32, one launch (start us, length us, event | category | flops | bytes accessed | tf_op | source)
XLA Modules:
  0.0 628.9 jit_solution(4961322047628718233)
XLA Ops:
  7.2 0.0 copy-start
  7.2 0.0 reduce-scatter.6.cloned.1.call-start
  7.2 22.2 %all_gather.10 = bf16[512,768]{1,0:T(8,128)(2,1)S(1)} all-gather(bf16[32,768]{1,0:T(8,128)(2,1)} %param.7), channel_id=1, replica_groups=mesh['row'=16,'col'=16] {'row'}, dimensions={0}, use_global_device_ids=true | all-gather | bytes 835584 | tf_op jit(solution)/shard_map/all_gather | solution.py:66
  29.4 0.0 copy-done
  29.5 0.0 copy-start.1
  29.5 3.0 fusion.45
  32.5 0.0 copy-done.1
  32.5 0.0 copy-start.2
  32.5 0.0 reduce-scatter.6.cloned.1.call-update
  32.5 0.0 reduce-scatter.4.cloned.1.call-start
  32.6 0.7 copy-done.2
  33.3 18.4 %all_gather.9 = bf16[512,768]{1,0:T(8,128)(2,1)S(1)} all-gather(bf16[32,768]{1,0:T(8,128)(2,1)S(1)} %copy-done.2), channel_id=1, replica_groups=mesh['row'=16,'col'=16] {'row'}, dimensions={0}, use_global_device_ids=true | all-gather | bytes 835584 | tf_op jit(solution)/shard_map/all_gather | solution.py:67
  51.7 4.8 fusion.44
  56.5 0.0 copy-start.3
  56.5 0.0 copy-start.4
  56.5 0.0 copy-start.5
  56.5 0.0 reduce-scatter.4.cloned.1.call-update
  56.5 0.6 copy-done.3
  57.1 0.6 fusion.43
  59.7 183.7 %reduce-scatter.6.cloned.1.call-done = f32[32,1536]{1,0:T(8,128)} async-done(((f32[512,1536]{1,0:T(8,128)}), f32[32,1536]{1,0:T(8,128)}) %reduce-scatter.6.cloned.1.call-update) | async-done | bytes 196624 | tf_op jit(solution)/shard_map/reduce_scatter | solution.py:75
  243.4 213.6 %reduce-scatter.4.cloned.1.call-done = f32[32,1536]{1,0:T(8,128)} async-done(((f32[512,1536]{1,0:T(8,128)}), f32[32,1536]{1,0:T(8,128)}) %reduce-scatter.4.cloned.1.call-update) | async-done | bytes 196624 | tf_op jit(solution)/shard_map/reduce_scatter | solution.py:76
  457.0 0.0 copy-done.4
  457.0 0.0 copy-done.5
  457.0 2.5 multiply_convert_fusion
  459.6 1.3 stack.2
  460.9 6.9 %all-to-all-start = ((bf16[16,32,1536]{2,1,0:T(8,128)(2,1)}), bf16[16,32,1536]{2,1,0:T(8,128)(2,1)}, u32[]{:S(2)}, u32[]{:S(2)}) async-start(bf16[16,32,1536]{2,1,0:T(8,128)(2,1)} %stack.2), calls=%async_computation.2 | async-start | bytes 3145728 | tf_op jit(solution)/shard_map/all_to_all | solution.py:93
  467.7 0.0 all-gather.2.cloned.1.call-start
  467.8 0.7 all-gather.2.cloned.1.call-update
  468.5 0.0 reduce-scatter.8.cloned.1.call-start
  468.5 36.2 %all-to-all-done = bf16[16,32,1536]{2,1,0:T(8,128)(2,1)} async-done(((bf16[16,32,1536]{2,1,0:T(8,128)(2,1)}), bf16[16,32,1536]{2,1,0:T(8,128)(2,1)}, u32[]{:S(2)}, u32[]{:S(2)}) %all-to-all-start) | async-done | bytes 1572896 | tf_op jit(solution)/shard_map/all_to_all | solution.py:93
  504.8 4.0 fusion.46
  508.7 0.0 reduce-scatter.8.cloned.1.call-update
  508.7 0.7 convert_reduce_fusion.1
  509.5 4.4 fusion
  513.9 4.3 copy.13
  518.2 2.3 convert_reduce_fusion
  520.5 35.2 %all-gather.2.cloned.1.call-done = bf16[512,1536]{1,0:T(8,128)(2,1)} async-done(((bf16[32,1536]{1,0:T(8,128)(2,1)}), bf16[512,1536]{1,0:T(8,128)(2,1)}) %all-gather.2.cloned.1.call-update) | async-done | bytes 1572880 | tf_op jit(solution)/shard_map/all_gather | solution.py:91
  555.6 4.2 convolution_convert_fusion
  559.9 61.0 %reduce-scatter.8.cloned.1.call-done = f32[32,768]{1,0:T(8,128)} async-done(((f32[512,768]{1,0:T(8,128)}), f32[32,768]{1,0:T(8,128)}) %reduce-scatter.8.cloned.1.call-update) | async-done | bytes 98320 | tf_op jit(solution)/shard_map/reduce_scatter | solution.py:108
  620.9 1.5 convert_element_type.29
  (2 shorter events, 0.0 us)
Async XLA Ops:
  7.2 22.3 %copy-start = (bf16[768,1536]{1,0:T(8,128)(2,1)S(1)}, bf16[768,1536]{1,0:T(8,128)(2,1)}, u32[]{:S(2)}) copy-start(bf16[768,1536]{1,0:T(8,128)(2,1)} %param.9) | copy-start | bytes 7077892
  7.2 236.2 %reduce-scatter.6.cloned.1.call-start = ((), (), s32[]{:S(2)}) async-start(), calls=%async_computation.5 | async-start | bytes 3342336 | tf_op jit(solution)/shard_map/reduce_scatter | solution.py:75
  29.5 3.0 copy-start.1
  32.5 0.8 copy-start.2
  32.5 424.5 %reduce-scatter.4.cloned.1.call-start = ((), (), s32[]{:S(2)}) async-start(), calls=%async_computation.4 | async-start | bytes 3342336 | tf_op jit(solution)/shard_map/reduce_scatter | solution.py:76
  56.5 0.7 copy-start.3
  56.5 400.6 %copy-start.4 = (s32[64,192]{1,0:T(8,128)S(1)}, s32[64,192]{1,0:T(8,128)}, u32[]{:S(2)}) copy-start(s32[64,192]{1,0:T(8,128)} %param.13) | copy-start | bytes 147460
  56.5 400.6 %copy-start.5 = (f32[1536]{0:T(1024)S(1)}, f32[1536]{0:T(1024)}, u32[]{:S(2)}) copy-start(f32[1536]{0:T(1024)} %param.11) | copy-start | bytes 18436
  460.9 43.9 %all-to-all-start = ((bf16[16,32,1536]{2,1,0:T(8,128)(2,1)}), bf16[16,32,1536]{2,1,0:T(8,128)(2,1)}, u32[]{:S(2)}, u32[]{:S(2)}) async-start(bf16[16,32,1536]{2,1,0:T(8,128)(2,1)} %stack.2), calls=%async_computation.2 | async-start | bytes 3145728 | tf_op jit(solution)/shard_map/all_to_all | solution.py:93
  467.7 87.9 %all-gather.2.cloned.1.call-start = ((), (), s32[]{:S(2)}) async-start(), calls=%async_computation.7 | async-start | bytes 1671168 | tf_op jit(solution)/shard_map/all_gather | solution.py:91
  468.5 152.4 %reduce-scatter.8.cloned.1.call-start = ((), (), s32[]{:S(2)}) async-start(), calls=%async_computation.6 | async-start | bytes 1671168 | tf_op jit(solution)/shard_map/reduce_scatter | solution.py:108
Sparse Core Ops, SparseCore 0:
  32.6 210.7 reduce-scatter.5
  247.4 209.5 reduce-scatter.3
  471.1 84.4 all-gather.1
  558.0 62.8 reduce-scatter.7
